TPU v7x, 32 devices: a whole 2x2x4 slice. The times are simulated.
32 devices in a mesh: sub: 8 (over z, y), grp: 4 (over x, core).
Axes of the slice: x: 2, y: 2, z: 4, core: 2. Of those that a mesh axis runs over, the one named last changes fastest.
Arguments:
- stiffness: bfloat16 [8, 64, 5, 256, 256], P('sub', 'grp'), may hold values from -0.0012207031 to 0.0012207031
- deflation: bfloat16 [8, 64, 16384], P('sub', None, 'grp'), may hold values from -6 to 6
- off_map: int32 [8, 3], replicated, may hold values from -2 to 2, as said below
- need_map: int32 [8, 4, 3, 4], P(None, 'grp'), may hold values from 0 to 15, as said below
- place_map: int32 [8, 4, 3, 4], P('sub', 'grp'), may hold values from 0 to 15, as said below
Outputs:
- coarse: float32 [8, 256, 256], P('sub', 'grp')
Inputs may be any that keep to these rules, and one draw needn't show every extreme that they name: `off_map`: the 3 offsets of one row are distinct and nonzero. `need_map`: the 4 tile numbers of one row are distinct. `place_map`: the 4 tile numbers of one row are distinct.
All inputs are finite; a program needn't handle non-finite values.
Results may differ from a plain program's by a relative error of at most 0.0029.
Values may be sent and summed in bfloat16 or wider, within the bound.
A program may use at most 128 MiB of HBM per device.

v0:
```python
import jax
import jax.numpy as jnp
from jax import lax
from jax.sharding import PartitionSpec as P

RCH = 2


def passed_along(value, axis, steps):
    count = lax.axis_size(axis)
    pairs = [(source, (source + steps) % count) for source in range(count)]
    return lax.ppermute(value, axis, pairs)


def with_halo(block, sides, width):
    for axis, dim in sides:
        count = lax.axis_size(axis)
        forward = [(i, i + 1) for i in range(count - 1)]
        backward = [(target, source) for source, target in forward]
        low = lax.ppermute(
            lax.slice_in_dim(block, block.shape[dim] - width, None, axis=dim), axis, forward
        )
        high = lax.ppermute(lax.slice_in_dim(block, 0, width, axis=dim), axis, backward)
        block = jnp.concatenate([low, block, high], axis=dim)
    return block


def slot_position(offset_value, reach_tiles):
    return jnp.where(offset_value > 0, offset_value + reach_tiles - 1, offset_value + reach_tiles)


def on_device(stiffness, deflation, off_map, need_map, place_map):
    sub_count = lax.axis_size("sub")
    my_index = lax.axis_index("sub")
    tile_count = stiffness.shape[1]
    band_count = stiffness.shape[2]
    tile_rows = stiffness.shape[3]
    vectors = deflation.shape[1]
    slot_count = off_map.shape[1]
    reach_tiles = RCH
    rim_tiles = band_count // 2
    own_tiles = deflation[0].reshape(vectors, tile_count, tile_rows)
    my_offsets = off_map[my_index]
    my_place = place_map[0, 0]
    offsets = [value for value in range(-reach_tiles, reach_tiles + 1) if value != 0]
    gathered = []
    arrived = {}
    for offset in offsets:
        target = jnp.mod(my_index + offset, sub_count)
        matched = off_map[target] == -offset
        has_match = jnp.any(matched)
        slot_pick = jnp.argmax(matched.astype(jnp.int32))
        wanted = need_map[target, 0][slot_pick]
        packed = jnp.take(own_tiles, wanted, axis=1) * has_match.astype(own_tiles.dtype)
        arrived[-offset] = passed_along(packed, "sub", offset)
    stacked = jnp.stack([arrived[value] for value in offsets], 0)
    for slot_index in range(slot_count):
        position = slot_position(my_offsets[slot_index], reach_tiles)
        gathered.append(lax.dynamic_index_in_dim(stacked, position, 0, keepdims=False))
    neighbour_blocks = []
    for slot_index in range(slot_count):
        blank_tiles = jnp.zeros((vectors, tile_count, tile_rows), own_tiles.dtype)
        neighbour_blocks.append(
            blank_tiles.at[:, my_place[slot_index], :].set(gathered[slot_index])
        )
    layered = jnp.concatenate([own_tiles] + neighbour_blocks, 0)
    padded = with_halo(layered, (("grp", 1),), rim_tiles)
    running = jnp.zeros(layered.shape, jnp.float32)
    for band_index in range(band_count):
        window = padded[:, band_index : band_index + tile_count]
        running = running + jnp.einsum(
            "ctk,tjk->ctj", window, stiffness[0, :, band_index], preferred_element_type=jnp.float32
        )
    product_image = running.astype(jnp.bfloat16)
    columns = layered.shape[0]
    flat_basis = layered.reshape(columns, -1)
    flat_image = product_image.reshape(columns, -1)
    share = lax.psum_scatter(
        lax.dot_general(
            flat_basis, flat_image, (((1,), (1,)), ((), ())), preferred_element_type=jnp.float32
        ),
        "grp",
        scatter_dimension=0,
        tiled=True,
    )
    return share[None]


def solution(mesh):
    in_specs = (
        P("sub", "grp", None, None, None),
        P("sub", None, "grp"),
        P(),
        P(None, "grp", None, None),
        P("sub", "grp", None, None),
    )
    out_specs = P("sub", "grp", None)
    return jax.shard_map(
        on_device, mesh=mesh, in_specs=in_specs, out_specs=out_specs, check_vma=False
    )
```

profile of v0, /device:TPU:0, one launch (start us, length us, event | category | flops | bytes accessed | tf_op | source)
XLA Modules:
  0.0 99.5 jit_solution(4612840696461299752)
XLA Ops:
  6.5 1.6 %fusion.46 = (pred[]{:T(512)}, pred[1,3]{0,1:T(4,128)(4,1)S(1)}, pred[]{:T(512)}, pred[1,3]{0,1:T(4,128)(4,1)S(1)}, pred[]{:T(512)}, /*index=5*/pred[1,3]{0,1:T(4,128)(4,1)S(1)}, pred[]{:T(512)}, pred[1,3]{0,1:T(4,128)(4,1)S(1)}) fusion(s32[8,3]{0,1:T(4,128)} %param.9, s32[]{:T(128)S(6)} %select_n.153, s32[]{:T(128)S(6)} %select_n.148, s32[]{:T(128)S(6)} %select_n.143, ...), kind=kLoop, calls=%fused_computation.89 | loop fusion | flops 20 | bytes 80 | tf_op jit(solution)/shard_map/reduce_or | solution.py:51
  8.3 0.7 iota_reduce_fusion
  10.4 0.7 iota_reduce_fusion.2
  12.4 0.7 iota_reduce_fusion.3
  14.3 0.7 iota_reduce_fusion.1
  18.5 1.5 %fusion.28 = (s32[4]{0:T(128)S(1)}, s32[4]{0:T(128)S(1)}, s32[4]{0:T(128)S(1)}, s32[4]{0:T(128)}) fusion(s32[8,1,3,4]{0,3,2,1:T(4,128)} %param.10, s32[]{:T(128)S(6)} %select_n.144, s32[]{:T(128)S(6)} %select_n.146, s32[]{:T(128)S(6)} %select_n.149, s32[]{:T(128)S(6)} %select_n.151, s32[]{:T(128)S(6)} %select_n.159, s32[]{:T(128)S(6)} %select_n.161, ...), kind=kLoop, calls=%fused_computation.61 | loop fusion | bytes 160 | tf_op jit(solution)/shard_map/dynamic_slice | solution.py:53
  20.7 1.2 %copy.22 = bf16[8,8,16,256]{3,2,1,0:T(8,128)(2,1)S(1)} copy(bf16[8,8,16,256]{3,1,2,0:T(8,128)(2,1)} %bitcast.87) | data formatting | bytes 1048576
  22.7 3.1 %collective-permute-start = (bf16[64,4,256]{2,0,1:T(8,128)(2,1)S(1)}, bf16[64,4,256]{2,0,1:T(8,128)(2,1)S(1)}, u32[]{:S(2)}, u32[]{:S(2)}) collective-permute-start(bf16[64,4,256]{2,0,1:T(8,128)(2,1)S(1)} %bitcast_multiply_fusion.3), channel_id=1, source_target_pairs={{0,8},{4,12},{8,16},{12,20},{16,24},{20,28},{24,0},{28,4},{1,9},{5... | collective-permute-start | bytes 393224 | tf_op jit(solution)/shard_map/ppermute | solution.py:12
  27.1 2.1 %collective-permute-start.3 = (bf16[64,4,256]{2,0,1:T(8,128)(2,1)S(1)}, bf16[64,4,256]{2,0,1:T(8,128)(2,1)S(1)}, u32[]{:S(2)}, u32[]{:S(2)}) collective-permute-start(bf16[64,4,256]{2,0,1:T(8,128)(2,1)S(1)} %bitcast_multiply_fusion), channel_id=1, source_target_pairs={{0,24},{4,28},{8,0},{12,4},{16,8},{20,12},{24,16},{28,20},{1,25},{... | collective-permute-start | bytes 393224 | tf_op jit(solution)/shard_map/ppermute | solution.py:12
  30.6 1.7 %collective-permute-start.1 = (bf16[64,4,256]{2,0,1:T(8,128)(2,1)S(1)}, bf16[64,4,256]{2,0,1:T(8,128)(2,1)S(1)}, u32[]{:S(2)}, u32[]{:S(2)}) collective-permute-start(bf16[64,4,256]{2,0,1:T(8,128)(2,1)S(1)} %bitcast_multiply_fusion.2), channel_id=1, source_target_pairs={{0,4},{4,8},{8,12},{12,16},{16,20},{20,24},{24,28},{28,0},{1,5},{5... | collective-permute-start | bytes 393224 | tf_op jit(solution)/shard_map/ppermute | solution.py:12
  32.4 0.7 compare_and_fusion.1
  33.1 0.7 compare_select_fusion.1
  35.1 3.1 %collective-permute-start.2 = (bf16[64,4,256]{2,0,1:T(8,128)(2,1)S(1)}, bf16[64,4,256]{2,0,1:T(8,128)(2,1)S(1)}, u32[]{:S(2)}, u32[]{:S(2)}) collective-permute-start(bf16[64,4,256]{2,0,1:T(8,128)(2,1)S(1)} %bitcast_multiply_fusion.1), channel_id=1, source_target_pairs={{0,28},{4,0},{8,4},{12,8},{16,12},{20,16},{24,20},{28,24},{1,29},{... | collective-permute-start | bytes 393224 | tf_op jit(solution)/shard_map/ppermute | solution.py:12
  44.8 0.6 scatter_fusion
  45.5 0.6 scatter_fusion.1
  46.3 0.6 scatter_fusion.2
  47.0 1.3 %collective-permute-start.5 = (bf16[256,2,256]{2,0,1:T(8,128)(2,1)S(1)}, bf16[256,2,256]{2,0,1:T(8,128)(2,1)S(1)}, u32[]{:S(2)}, u32[]{:S(2)}) collective-permute-start(bf16[256,2,256]{2,0,1:T(8,128)(2,1)S(1)} %get-tuple-element.27), channel_id=1, source_target_pairs={{1,0},{2,1},{3,2},{5,4},{6,5},{7,6},{9,8},{10,9},{11,10},{13,12},{... | collective-permute-start | bytes 786440 | tf_op jit(solution)/shard_map/ppermute | solution.py:23
  48.4 3.4 %collective-permute-start.4 = (bf16[256,2,256]{2,0,1:T(8,128)(2,1)S(1)}, bf16[256,2,256]{2,0,1:T(8,128)(2,1)S(1)}, u32[]{:S(2)}, u32[]{:S(2)}) collective-permute-start(bf16[256,2,256]{2,0,1:T(8,128)(2,1)S(1)} %get-tuple-element.26), channel_id=1, source_target_pairs={{0,1},{1,2},{2,3},{4,5},{5,6},{6,7},{8,9},{9,10},{10,11},{12,13},{... | collective-permute-start | bytes 786440 | tf_op jit(solution)/shard_map/ppermute | solution.py:20
  51.8 4.3 %fusion.3 = f32[16,256,256]{2,1,0:T(8,128)} fusion(bf16[1,16,5,256,256]{4,3,2,1,0:T(8,128)(2,1)} %param.7, bf16[256,2,256]{2,0,1:T(8,128)(2,1)S(1)} %collective-permute-done.5, bf16[256,16,256]{2,0,1:T(8,128)(2,1)S(1)} %constant_dynamic-update-slice_fusion), kind=kOutput, calls=%fused_computation.12 | convolution fusion | flops 541589504 | bytes 8650752 | tf_op jit(solution)/shard_map/ctk,tjk->ctj/dot_general | solution.py:71
  56.1 2.7 %fusion.5 = f32[16,256,256]{2,1,0:T(8,128)} fusion(bf16[1,16,5,256,256]{4,3,2,1,0:T(8,128)(2,1)S(1)} %bitcast.89, bf16[256,2,256]{2,0,1:T(8,128)(2,1)S(1)} %collective-permute-done.5, bf16[256,16,256]{2,0,1:T(8,128)(2,1)S(1)} %constant_dynamic-update-slice_fusion), kind=kOutput, calls=%fused_computation.14 | convolution fusion | flops 541589504 | bytes 8650752 | tf_op jit(solution)/shard_map/ctk,tjk->ctj/dot_general | solution.py:71
  58.8 2.7 %fusion.9 = f32[16,256,256]{2,1,0:T(8,128)} fusion(bf16[1,16,5,256,256]{4,3,2,1,0:T(8,128)(2,1)S(1)} %bitcast.89, bf16[256,16,256]{2,0,1:T(8,128)(2,1)S(1)} %constant_dynamic-update-slice_fusion, bf16[256,2,256]{2,0,1:T(8,128)(2,1)S(1)} %collective-permute-done.4), kind=kOutput, calls=%fused_computation.18 | convolution fusion | flops 541589504 | bytes 8650752 | tf_op jit(solution)/shard_map/ctk,tjk->ctj/dot_general | solution.py:71
  61.5 2.7 %fusion.11 = f32[16,256,256]{2,1,0:T(8,128)} fusion(bf16[1,16,5,256,256]{4,3,2,1,0:T(8,128)(2,1)S(1)} %bitcast.89, bf16[256,16,256]{2,0,1:T(8,128)(2,1)S(1)} %constant_dynamic-update-slice_fusion, bf16[256,2,256]{2,0,1:T(8,128)(2,1)S(1)} %collective-permute-done.4), kind=kOutput, calls=%fused_computation.20 | convolution fusion | flops 541589504 | bytes 8650752 | tf_op jit(solution)/shard_map/ctk,tjk->ctj/dot_general | solution.py:71
  64.3 8.6 %fusion.22 = f32[256,256]{1,0:T(8,128)} fusion(bf16[256,16,256]{2,0,1:T(8,128)(2,1)S(1)} %constant_dynamic-update-slice_fusion, f32[16,256,256]{2,1,0:T(8,128)} %fusion.3, f32[16,256,256]{2,1,0:T(8,128)} %fusion.5, f32[16,256,256]{2,1,0:T(8,128)} %fusion.11, f32[16,256,256]{2,1,0:T(8,128)} %fusion.9, bf16[1,16,5,256,256]{4,3,2,1,0:T(8,128)(2,1)} %param.7), kind=kOutput, calls=%fused_computation.27 | convolution fusion | flops 1078984704 | bytes 23330816 | tf_op jit(solution)/shard_map/dot_general | solution.py:79
  72.9 19.8 %reduce-scatter.2.cloned.1.call-done = f32[64,256]{1,0:T(8,128)} async-done(((f32[256,256]{1,0:T(8,128)}), f32[64,256]{1,0:T(8,128)}) %reduce-scatter.2.cloned.1.call-update) | async-done | bytes 65552 | tf_op jit(solution)/shard_map/reduce_scatter | solution.py:78
  (52 shorter events, 4.3 us)
Async XLA Ops:
  6.5 86.1 %reduce-scatter.2.cloned.1.call-start = ((), (), s32[]{:S(2)}) async-start(), calls=%async_computation.1 | async-start | bytes 327680 | tf_op jit(solution)/shard_map/reduce_scatter | solution.py:78
  20.7 17.5 %copy-start = (s32[8,3]{0,1:T(4,128)S(1)}, s32[8,3]{0,1:T(4,128)}, u32[]{:S(2)}) copy-start(s32[8,3]{0,1:T(4,128)} %param.9) | copy-start | bytes 292
  20.7 23.9 %copy-start.1 = (s32[1,1,3,4]{3,1,2,0:T(1,128)S(1)}, s32[1,1,3,4]{3,1,2,0:T(1,128)}, u32[]{:S(2)}) copy-start(s32[1,1,3,4]{3,1,2,0:T(1,128)} %param.11) | copy-start | bytes 148
  22.7 21.8 %collective-permute-start = (bf16[64,4,256]{2,0,1:T(8,128)(2,1)S(1)}, bf16[64,4,256]{2,0,1:T(8,128)(2,1)S(1)}, u32[]{:S(2)}, u32[]{:S(2)}) collective-permute-start(bf16[64,4,256]{2,0,1:T(8,128)(2,1)S(1)} %bitcast_multiply_fusion.3), channel_id=1, source_target_pairs={{0,8},{4,12},{8,16},{12,20},{16,24},{20,28},{24,0},{28,4},{1,9},{5... | collective-permute-start | bytes 393224 | tf_op jit(solution)/shard_map/ppermute | solution.py:12
  27.1 17.4 %collective-permute-start.3 = (bf16[64,4,256]{2,0,1:T(8,128)(2,1)S(1)}, bf16[64,4,256]{2,0,1:T(8,128)(2,1)S(1)}, u32[]{:S(2)}, u32[]{:S(2)}) collective-permute-start(bf16[64,4,256]{2,0,1:T(8,128)(2,1)S(1)} %bitcast_multiply_fusion), channel_id=1, source_target_pairs={{0,24},{4,28},{8,0},{12,4},{16,8},{20,12},{24,16},{28,20},{1,25},{... | collective-permute-start | bytes 393224 | tf_op jit(solution)/shard_map/ppermute | solution.py:12
  30.6 13.9 %collective-permute-start.1 = (bf16[64,4,256]{2,0,1:T(8,128)(2,1)S(1)}, bf16[64,4,256]{2,0,1:T(8,128)(2,1)S(1)}, u32[]{:S(2)}, u32[]{:S(2)}) collective-permute-start(bf16[64,4,256]{2,0,1:T(8,128)(2,1)S(1)} %bitcast_multiply_fusion.2), channel_id=1, source_target_pairs={{0,4},{4,8},{8,12},{12,16},{16,20},{20,24},{24,28},{28,0},{1,5},{5... | collective-permute-start | bytes 393224 | tf_op jit(solution)/shard_map/ppermute | solution.py:12
  35.1 9.5 %collective-permute-start.2 = (bf16[64,4,256]{2,0,1:T(8,128)(2,1)S(1)}, bf16[64,4,256]{2,0,1:T(8,128)(2,1)S(1)}, u32[]{:S(2)}, u32[]{:S(2)}) collective-permute-start(bf16[64,4,256]{2,0,1:T(8,128)(2,1)S(1)} %bitcast_multiply_fusion.1), channel_id=1, source_target_pairs={{0,28},{4,0},{8,4},{12,8},{16,12},{20,16},{24,20},{28,24},{1,29},{... | collective-permute-start | bytes 393224 | tf_op jit(solution)/shard_map/ppermute | solution.py:12
  47.0 4.8 %collective-permute-start.5 = (bf16[256,2,256]{2,0,1:T(8,128)(2,1)S(1)}, bf16[256,2,256]{2,0,1:T(8,128)(2,1)S(1)}, u32[]{:S(2)}, u32[]{:S(2)}) collective-permute-start(bf16[256,2,256]{2,0,1:T(8,128)(2,1)S(1)} %get-tuple-element.27), channel_id=1, source_target_pairs={{1,0},{2,1},{3,2},{5,4},{6,5},{7,6},{9,8},{10,9},{11,10},{13,12},{... | collective-permute-start | bytes 786440 | tf_op jit(solution)/shard_map/ppermute | solution.py:23
  48.3 7.8 %slice-start = ((s8[10485760]{0:T(1024)(128)(4,1)}), s8[4194304]{0:T(1024)(128)(4,1)S(1)}, s32[]{:S(2)}) async-start(s8[10485760]{0:T(1024)(128)(4,1)} %bitcast.88), calls=%async_computation.2 | async-start | bytes 8388608
  48.3 7.8 %slice-start.1 = ((s8[10485760]{0:T(1024)(128)(4,1)}), s8[4194304]{0:T(1024)(128)(4,1)S(1)}, s32[]{:S(2)}) async-start(s8[10485760]{0:T(1024)(128)(4,1)} %bitcast.88), calls=%async_computation.3 | async-start | bytes 8388608
  48.4 7.7 %slice-start.2 = ((s8[10485760]{0:T(1024)(128)(4,1)}), s8[2097152]{0:T(1024)(128)(4,1)S(1)}, s32[]{:S(2)}) async-start(s8[10485760]{0:T(1024)(128)(4,1)} %bitcast.88), calls=%async_computation.4 | async-start | bytes 4194304
  48.4 10.5 %collective-permute-start.4 = (bf16[256,2,256]{2,0,1:T(8,128)(2,1)S(1)}, bf16[256,2,256]{2,0,1:T(8,128)(2,1)S(1)}, u32[]{:S(2)}, u32[]{:S(2)}) collective-permute-start(bf16[256,2,256]{2,0,1:T(8,128)(2,1)S(1)} %get-tuple-element.26), channel_id=1, source_target_pairs={{0,1},{1,2},{2,3},{4,5},{5,6},{6,7},{8,9},{9,10},{10,11},{12,13},{... | collective-permute-start | bytes 786440 | tf_op jit(solution)/shard_map/ppermute | solution.py:20
Sparse Core Ops, SparseCore 0:
  73.0 19.6 reduce-scatter.1
where the time goes:
time: 100 us; the launch traced here: 99.5 us
  between operations  29.3 us (29%)
  matrix products  21 us (21%)
  waiting for transfers between devices  19.8 us (20%)
  starting transfers between devices  14.8 us (15%)
  local copies, waits for them, and re-layouts  8.09 us (8%)
  other arithmetic  6.52 us (7%)
    reduce_scatter x1, waiting for transfers between devices, on_device(): lax.psum_scatter(lax.dot_general(flat_basis, flat_image, (((1,), (1,)), (...  19.8 us
    dot_general x4, matrix products, on_device(): jnp.einsum('ctk,tjk->ctj', window, stiffness[0, :, band_index], preferred...  12.4 us
    ppermute x4, starting transfers between devices, passed_along(): return lax.ppermute(value, axis, pairs)  10.1 us
    dot_general x1, matrix products, on_device(): lax.dot_general(flat_basis, flat_image, (((1,), (1,)), ((), ())), preferr...  8.59 us
    ppermute x1, starting transfers between devices, with_halo(): lax.ppermute(lax.slice_in_dim(block, block.shape[dim] - width, None, axis...  3.44 us
    another operation x4, other arithmetic, on_device(): slot_pick = jnp.argmax(matched.astype(jnp.int32))  2.8 us
    gather x4, local copies, waits for them, and re-layouts, on_device(): jnp.take(own_tiles, wanted, axis=1) * has_match.astype(own_tiles.dtype)  2.22 us
  transfers between devices with their start and end apart: 7, of which 1 were waited for; matrix products, arithmetic and copies ran while one was open for 11% of the time, Pallas kernels for 0%

commit v1 on v0

v1 whole, which is shorter than its diff:
```python
import functools

import jax
import jax.numpy as jnp
from jax import lax
from jax.experimental import pallas as pl
from jax.experimental.pallas import tpu as pltpu
from jax.sharding import PartitionSpec as P

RCH = 2
MESH = pl.DeviceIdType.MESH
OFFSETS = [value for value in range(-RCH, RCH + 1) if value != 0]
NT = (((1,), (1,)), ((), ()))


def dot_nt(lhs, rhs):
    return lax.dot_general(lhs, rhs, NT, preferred_element_type=jnp.float32)


def kernel(
    subs, layers, off_ref, need_ref, place_ref, defl_ref, stiff_ref, out_ref,
    a_buf, basis, image, own_tiles, outgoing, arrived, part, part_low, shares,
    a_sem, sub_send, sub_recv, own_send, own_recv, rim_send, rim_recv, red_send, red_recv,
):
    s = lax.axis_index("sub")
    g = lax.axis_index("grp")
    _, tiles, bands, rows, _ = stiff_ref.shape
    vectors = defl_ref.shape[1]
    slots = off_ref.shape[0]
    overlap = place_ref.shape[3]
    rim = bands // 2
    halo = rim * rows
    width = tiles * rows
    columns = vectors * (slots + 1)
    share = out_ref.shape[1]
    has_left = g > 0
    has_right = g < layers - 1

    def stiff_copy(t):
        return pltpu.make_async_copy(stiff_ref.at[0, t], a_buf.at[t], a_sem.at[t])

    edge_low = list(range(rim))
    edge_high = list(range(tiles - rim, tiles))
    interior = list(range(rim, tiles - rim))

    barrier = pltpu.get_barrier_semaphore()
    for offset in OFFSETS:
        pl.semaphore_signal(
            barrier, inc=1, device_id=(lax.rem(s + offset + subs, subs), g), device_id_type=MESH
        )
    for step in range(1, layers):
        pl.semaphore_signal(
            barrier, inc=1, device_id=(s, lax.rem(g + step, layers)), device_id_type=MESH
        )
    for t in interior + edge_low + edge_high:
        stiff_copy(t).start()

    for u in range(tiles):
        own_tiles[u] = defl_ref[0, :, u * rows : (u + 1) * rows]
    for k, offset in enumerate(OFFSETS):
        target = lax.rem(s + offset + subs, subs)
        for o in range(overlap):
            tile = jnp.int32(0)
            for n in range(slots):
                match = (off_ref[n, target] == -offset).astype(jnp.int32)
                tile = tile + match * need_ref[0, n, o, target]
            outgoing[k, o] = own_tiles[tile]
    for k in range(len(OFFSETS)):
        arrived[k * (overlap + 1) + overlap] = jnp.zeros((vectors, rows), arrived.dtype)
    basis[0:vectors, halo : halo + width] = defl_ref[0]

    @pl.when(jnp.logical_not(has_left))
    def _():
        basis[:, 0:halo] = jnp.zeros((columns, halo), basis.dtype)

    @pl.when(jnp.logical_not(has_right))
    def _():
        basis[:, halo + width :] = jnp.zeros((columns, halo), basis.dtype)

    pl.semaphore_wait(barrier, len(OFFSETS) + layers - 1)

    count = len(OFFSETS)
    sub_copies = []
    for k, offset in enumerate(OFFSETS):
        sub_copies.append(
            pltpu.make_async_remote_copy(
                src_ref=outgoing.at[k],
                dst_ref=arrived.at[pl.ds((count - 1 - k) * (overlap + 1), overlap)],
                send_sem=sub_send.at[k],
                recv_sem=sub_recv.at[count - 1 - k],
                device_id=(lax.rem(s + offset + subs, subs), g),
                device_id_type=MESH,
            )
        )
    for copy in sub_copies:
        copy.start()

    def own_left():
        return pltpu.make_async_remote_copy(
            src_ref=defl_ref.at[0, :, pl.ds(0, halo)],
            dst_ref=basis.at[pl.ds(0, vectors), pl.ds(halo + width, halo)],
            send_sem=own_send.at[0],
            recv_sem=own_recv.at[1],
            device_id=(s, g - 1),
            device_id_type=MESH,
        )

    def own_right():
        return pltpu.make_async_remote_copy(
            src_ref=defl_ref.at[0, :, pl.ds(width - halo, halo)],
            dst_ref=basis.at[pl.ds(0, vectors), pl.ds(0, halo)],
            send_sem=own_send.at[1],
            recv_sem=own_recv.at[0],
            device_id=(s, g + 1),
            device_id_type=MESH,
        )

    def rim_left():
        return pltpu.make_async_remote_copy(
            src_ref=basis.at[pl.ds(vectors, columns - vectors), pl.ds(halo, halo)],
            dst_ref=basis.at[pl.ds(vectors, columns - vectors), pl.ds(halo + width, halo)],
            send_sem=rim_send.at[0],
            recv_sem=rim_recv.at[1],
            device_id=(s, g - 1),
            device_id_type=MESH,
        )

    def rim_right():
        return pltpu.make_async_remote_copy(
            src_ref=basis.at[pl.ds(vectors, columns - vectors), pl.ds(width, halo)],
            dst_ref=basis.at[pl.ds(vectors, columns - vectors), pl.ds(0, halo)],
            send_sem=rim_send.at[1],
            recv_sem=rim_recv.at[0],
            device_id=(s, g + 1),
            device_id_type=MESH,
        )

    def start_pair(left, right):
        @pl.when(has_left)
        def _():
            left().start()

        @pl.when(has_right)
        def _():
            right().start()

    def wait_pair(left, right):
        @pl.when(has_left)
        def _():
            right().wait_recv()
            left().wait_send()

        @pl.when(has_right)
        def _():
            left().wait_recv()
            right().wait_send()

    start_pair(own_left, own_right)

    def image_of(t, low, high):
        running = None
        for b in range(bands):
            start = (t + b) * rows
            if not isinstance(t, int):
                start = pl.multiple_of(start, rows)
            term = dot_nt(basis[low:high, pl.ds(start, rows)], a_buf[t, b])
            running = term if running is None else running + term
        at = t * rows if isinstance(t, int) else pl.multiple_of(t * rows, rows)
        image[low:high, pl.ds(at, rows)] = running.astype(image.dtype)

    def own_step(t, carry):
        stiff_copy(t).wait()
        image_of(t, 0, vectors)
        return carry

    lax.fori_loop(rim, tiles - rim, own_step, 0)
    wait_pair(own_left, own_right)
    for t in edge_low + edge_high:
        stiff_copy(t).wait()
        image_of(t, 0, vectors)

    for copy in sub_copies:
        copy.wait()

    def place(u, n):
        offset = off_ref[n, s]
        position = offset + RCH - (offset > 0).astype(jnp.int32)
        where_from = position * (overlap + 1) + overlap
        for o in range(overlap):
            hit = (place_ref[0, n, 0, o] == u).astype(jnp.int32)
            where_from = where_from + (o - overlap) * hit
        at = halo + u * rows
        if not isinstance(u, int):
            at = pl.multiple_of(at, rows)
        basis[(n + 1) * vectors : (n + 2) * vectors, pl.ds(at, rows)] = arrived[where_from]

    for u in edge_low + edge_high:
        for n in range(slots):
            place(u, n)

    def place_step(u, carry):
        for n in range(slots):
            place(u, n)
        return carry

    start_pair(rim_left, rim_right)
    lax.fori_loop(rim, tiles - rim, place_step, 0)

    def rest_step(t, carry):
        image_of(t, vectors, columns)
        return carry

    lax.fori_loop(rim, tiles - rim, rest_step, 0, unroll=2)
    inner = (tiles - 2 * rim) * rows
    part[...] = dot_nt(basis[:, 2 * halo : 2 * halo + inner], image[:, halo : halo + inner])

    wait_pair(rim_left, rim_right)
    for t in edge_low + edge_high:
        image_of(t, vectors, columns)
    total = part[...]
    total = total + dot_nt(basis[:, halo : 2 * halo], image[:, 0:halo])
    total = total + dot_nt(basis[:, width : width + halo], image[:, width - halo :])
    part[...] = total
    part_low[...] = total.astype(part_low.dtype)

    red_copies = []
    for step in range(1, layers):
        peer = lax.rem(g + step, layers)
        red_copies.append(
            pltpu.make_async_remote_copy(
                src_ref=part_low.at[pl.ds(pl.multiple_of(peer * share, share), share)],
                dst_ref=shares.at[step - 1],
                send_sem=red_send.at[step - 1],
                recv_sem=red_recv.at[step - 1],
                device_id=(s, peer),
                device_id_type=MESH,
            )
        )
    for copy in red_copies:
        copy.start()
    for copy in red_copies:
        copy.wait()
    result = part[pl.ds(pl.multiple_of(g * share, share), share), :]
    for step in range(1, layers):
        result = result + shares[step - 1].astype(jnp.float32)
    out_ref[0] = result


def on_device(subs, layers, stiffness, deflation, off_map, need_map, place_map):
    _, tiles, bands, rows, _ = stiffness.shape
    _, vectors, width = deflation.shape
    slots, overlap = place_map.shape[2:]
    columns = vectors * (slots + 1)
    halo = (bands // 2) * rows
    share = columns // layers
    count = len(OFFSETS)
    low = deflation.dtype
    dma = pltpu.SemaphoreType.DMA
    smem = pl.BlockSpec(memory_space=pltpu.SMEM)
    return pl.pallas_call(
        functools.partial(kernel, subs, layers),
        out_shape=jax.ShapeDtypeStruct((1, share, columns), jnp.float32),
        in_specs=[
            smem, smem, smem,
            pl.BlockSpec(memory_space=pltpu.VMEM),
            pl.BlockSpec(memory_space=pl.ANY),
        ],
        out_specs=pl.BlockSpec(memory_space=pltpu.VMEM),
        scratch_shapes=[
            pltpu.VMEM((tiles, bands, rows, rows), low),
            pltpu.VMEM((columns, width + 2 * halo), low),
            pltpu.VMEM((columns, width), low),
            pltpu.VMEM((tiles, vectors, rows), low),
            pltpu.VMEM((count, overlap, vectors, rows), low),
            pltpu.VMEM((count * (overlap + 1), vectors, rows), low),
            pltpu.VMEM((columns, columns), jnp.float32),
            pltpu.VMEM((columns, columns), low),
            pltpu.VMEM((layers - 1, share, columns), low),
            dma((tiles,)),
            dma((count,)), dma((count,)),
            dma((2,)), dma((2,)),
            dma((2,)), dma((2,)),
            dma((layers - 1,)), dma((layers - 1,)),
        ],
        compiler_params=pltpu.CompilerParams(collective_id=0, has_side_effects=True),
    )(
        off_map.T,
        need_map.transpose(1, 2, 3, 0),
        place_map.transpose(0, 2, 1, 3),
        deflation,
        stiffness,
    )


def solution(mesh):
    in_specs = (
        P("sub", "grp", None, None, None),
        P("sub", None, "grp"),
        P(),
        P(None, "grp", None, None),
        P("sub", "grp", None, None),
    )
    out_specs = P("sub", "grp", None)
    return jax.shard_map(
        functools.partial(on_device, mesh.shape["sub"], mesh.shape["grp"]),
        mesh=mesh,
        in_specs=in_specs,
        out_specs=out_specs,
        check_vma=False,
    )
```

time: 100 us -> 28.7 us (0.29)
  between operations: 29.3 us -> 0.01 us
  Pallas kernels: 0 us -> 27.1 us
  matrix products: 21 us -> 0 us
  waiting for transfers between devices: 19.8 us -> 0 us
  starting transfers between devices: 14.8 us -> 0 us
  local copies, waits for them, and re-layouts: 8.09 us -> 1.47 us
  other arithmetic: 6.52 us -> 0 us
    pallas_call x0 -> x1, Pallas kernels: none -> 27.1 us  [on_device(): pl.pallas_call(functools.partial(kernel, subs, layers), out_shape=jax.Sha...]
    dot_general x5 -> x0, matrix products: 21 us -> none  [the longest x4 12.4 us: on_device(): jnp.einsum('ctk,tjk->ctj', window, stiffness[0, :, band_index], preferred...]
    reduce_scatter x1 -> x0, waiting for transfers between devices: 19.8 us -> none  [on_device(): lax.psum_scatter(lax.dot_general(flat_basis, flat_image, (((1,), (1,)), (...]
    ppermute x6 -> x0, starting transfers between devices: 14.8 us -> none  [the longest x4 10.1 us: passed_along(): return lax.ppermute(value, axis, pairs)]
    another operation x5 -> x0, other arithmetic: 2.87 us -> none  [the longest x4 2.8 us: on_device(): slot_pick = jnp.argmax(matched.astype(jnp.int32))]
    gather x4 -> x0, local copies, waits for them, and re-layouts: 2.22 us -> none  [on_device(): jnp.take(own_tiles, wanted, axis=1) * has_match.astype(own_tiles.dtype)]
    scatter x3 -> x0, local copies, waits for them, and re-layouts: 1.94 us -> none  [on_device(): blank_tiles.at[:, my_place[slot_index], :].set(gathered[slot_index])]
    reduce_or x1 -> x0, other arithmetic: 1.62 us -> none  [on_device(): has_match = jnp.any(matched)]
  transfers between devices with their start and end apart: 7 -> 0, of which waited for: 1 -> 0; matrix products, arithmetic and copies ran while one was open for 11% -> 0% of each run, Pallas kernels for 0% -> 0%
where the time goes in v1:
time: 28.7 us; the launch traced here: 28.6 us
  Pallas kernels  27.1 us (94%)
  local copies, waits for them, and re-layouts  1.47 us (5%)
    pallas_call x1, Pallas kernels, on_device(): pl.pallas_call(functools.partial(kernel, subs, layers), out_shape=jax.Sha...  27.1 us
    unnamed x1, local copies, waits for them, and re-layouts  1.47 us

profile of v1, /device:TPU:0, one launch (start us, length us, event | category | flops | bytes accessed | tf_op | source)
XLA Modules:
  0.0 28.6 jit_solution(6296322003866046822)
XLA Ops:
  0.0 27.1 %shard_map.55 = f32[1,64,256]{2,1,0:T(8,128)} custom-call(s32[3,8]{1,0:T(4,128)} %bitcast.4, s32[1,3,4,8]{3,2,1,0:T(4,128)} %bitcast.3, s32[1,3,1,4]{3,2,1,0:T(1,128)} %bitcast.5, bf16[1,64,4096]{2,1,0:T(8,128)(2,1)} %defl_ref.1, bf16[1,16,5,256,256]{4,3,2,1,0:T(8,128)(2,1)} %stiff_ref.1), custom_call_target="tpu_custom_call" | custom-call | tf_op jit(solution)/shard_map/pallas_call | solution.py:260
  27.1 1.5 %copy.7 = f32[1,64,256]{2,1,0:T(8,128)} copy(f32[1,64,256]{2,1,0:T(8,128)} %shard_map.55) | data formatting | bytes 131072

commit v2 on v1

v2 whole, which is shorter than its diff:
```python
import functools

import jax
import jax.numpy as jnp
from jax import lax
from jax.experimental import pallas as pl
from jax.experimental.pallas import tpu as pltpu
from jax.sharding import PartitionSpec as P

RCH = 2
MESH = pl.DeviceIdType.MESH
OFFSETS = [value for value in range(-RCH, RCH + 1) if value != 0]
SEND_ORDER = sorted(OFFSETS, key=lambda value: (value < 0, abs(value)))
CHUNKS = 1
NT = (((1,), (1,)), ((), ()))


def dot_nt(lhs, rhs):
    return lax.dot_general(lhs, rhs, NT, preferred_element_type=jnp.float32)


def kernel(
    subs, layers, chunks, off_hbm, need_hbm, place_hbm, defl_ref, stiff_ref, out_ref,
    off_ref, need_ref, place_ref, a_buf, basis, image, own_tiles, outgoing, part, part_low, shares,
    in_sem, a_sem, sub_send, sub_recv, own_send, own_recv, rim_send, rim_recv, red_send, red_recv,
    *arrived,
):
    s = lax.axis_index("sub")
    g = lax.axis_index("grp")
    _, tiles, bands, rows, _ = stiff_ref.shape
    vectors = defl_ref.shape[1]
    slots = off_ref.shape[0]
    overlap = place_ref.shape[3]
    rim = bands // 2
    halo = rim * rows
    width = tiles * rows
    columns = vectors * (slots + 1)
    share = out_ref.shape[1]
    depth = vectors // chunks
    count = len(OFFSETS)
    has_left = g > 0
    has_right = g < layers - 1

    barrier = pltpu.get_barrier_semaphore()
    for offset in SEND_ORDER:
        pl.semaphore_signal(
            barrier, inc=1, device_id=(lax.rem(s + offset + subs, subs), g), device_id_type=MESH
        )
    for step in range(1, layers):
        pl.semaphore_signal(
            barrier, inc=1, device_id=(s, lax.rem(g + step, layers)), device_id_type=MESH
        )

    inputs = [
        pltpu.make_async_copy(off_hbm, off_ref, in_sem.at[0]),
        pltpu.make_async_copy(need_hbm, need_ref, in_sem.at[1]),
        pltpu.make_async_copy(place_hbm, place_ref, in_sem.at[2]),
        pltpu.make_async_copy(
            defl_ref.at[0], basis.at[0, :, pl.ds(halo, width)], in_sem.at[3]
        ),
    ]
    for copy in inputs:
        copy.start()

    def stiff_copy(t):
        return pltpu.make_async_copy(stiff_ref.at[0, t], a_buf.at[t], a_sem.at[t])

    edges = list(range(rim)) + list(range(tiles - rim, tiles))
    for t in list(range(rim, tiles - rim)) + edges:
        stiff_copy(t).start()

    for buffer in arrived:
        for k in range(count):
            buffer[k * (overlap + 1) + overlap] = jnp.zeros((depth, rows), buffer.dtype)

    @pl.when(jnp.logical_not(has_left))
    def _():
        basis[:, :, 0:halo] = jnp.zeros((slots + 1, vectors, halo), basis.dtype)

    @pl.when(jnp.logical_not(has_right))
    def _():
        basis[:, :, halo + width :] = jnp.zeros((slots + 1, vectors, halo), basis.dtype)

    for copy in inputs:
        copy.wait()
    for u in range(tiles):
        own_tiles[u] = basis[0, :, halo + u * rows : halo + (u + 1) * rows]
    for k, offset in enumerate(OFFSETS):
        target = lax.rem(s + offset + subs, subs)
        for o in range(overlap):
            tile = jnp.int32(0)
            for n in range(slots):
                match = (off_ref[n, target] == -offset).astype(jnp.int32)
                tile = tile + match * need_ref[0, n, o, target]
            outgoing[k, o] = own_tiles[tile]

    pl.semaphore_wait(barrier, count + layers - 1)

    def sub_copy(k, h):
        back = count - 1 - k
        return pltpu.make_async_remote_copy(
            src_ref=outgoing.at[k, :, pl.ds(h * depth, depth)],
            dst_ref=arrived[h].at[pl.ds(back * (overlap + 1), overlap)],
            send_sem=sub_send.at[h, k],
            recv_sem=sub_recv.at[h, back],
            device_id=(lax.rem(s + OFFSETS[k] + subs, subs), g),
            device_id_type=MESH,
        )

    for h in range(chunks):
        for offset in SEND_ORDER:
            sub_copy(OFFSETS.index(offset), h).start()

    def edge_copy(blocks, lines, to_left, send, recv):
        source, target = (halo, halo + width) if to_left else (width, 0)
        return pltpu.make_async_remote_copy(
            src_ref=basis.at[blocks, lines, pl.ds(source, halo)],
            dst_ref=basis.at[blocks, lines, pl.ds(target, halo)],
            send_sem=send.at[0 if to_left else 1],
            recv_sem=recv.at[1 if to_left else 0],
            device_id=(s, g - 1 if to_left else g + 1),
            device_id_type=MESH,
        )

    def own_copy(to_left):
        return edge_copy(pl.ds(0, 1), pl.ds(0, vectors), to_left, own_send, own_recv)

    def rim_copy(h):
        return lambda to_left: edge_copy(
            pl.ds(1, slots), pl.ds(h * depth, depth), to_left, rim_send.at[h], rim_recv.at[h]
        )

    def start_pair(make):
        @pl.when(has_left)
        def _():
            make(True).start()

        @pl.when(has_right)
        def _():
            make(False).start()

    def wait_pair(make):
        @pl.when(has_left)
        def _():
            make(False).wait_recv()
            make(True).wait_send()

        @pl.when(has_right)
        def _():
            make(True).wait_recv()
            make(False).wait_send()

    start_pair(own_copy)

    def column(t):
        return t * rows if isinstance(t, int) else pl.multiple_of(t * rows, rows)

    def image_of(t, blocks, lines):
        running = None
        for b in range(bands):
            window = basis[blocks, lines, pl.ds(column(t + b), rows)]
            shape = window.shape
            term = dot_nt(window.reshape(-1, rows), a_buf[t, b])
            running = term if running is None else running + term
        image[blocks, lines, pl.ds(column(t), rows)] = running.astype(image.dtype).reshape(shape)

    def own_step(t, carry):
        stiff_copy(t).wait()
        image_of(t, slice(0, 1), slice(0, vectors))
        return carry

    lax.fori_loop(rim, tiles - rim, own_step, 0, unroll=2)
    wait_pair(own_copy)
    for t in edges:
        stiff_copy(t).wait()
        image_of(t, slice(0, 1), slice(0, vectors))

    def place(h, u, n):
        offset = off_ref[n, s]
        position = offset + RCH - (offset > 0).astype(jnp.int32)
        found = position * (overlap + 1) + overlap
        for o in range(overlap):
            hit = (place_ref[0, n, 0, o] == u).astype(jnp.int32)
            found = found + (o - overlap) * hit
        lines = slice(h * depth, (h + 1) * depth)
        basis[n + 1, lines, pl.ds(halo + column(u), rows)] = arrived[h][found]

    for h in range(chunks):
        lines = slice(h * depth, (h + 1) * depth)
        for k in range(count):
            sub_copy(k, h).wait_recv()
        for u in edges:
            for n in range(slots):
                place(h, u, n)

        def place_step(u, carry):
            for n in range(slots):
                place(h, u, n)
            return carry

        lax.fori_loop(rim, tiles - rim, place_step, 0)
        start_pair(rim_copy(h))

        def rest_step(t, carry):
            image_of(t, slice(1, slots + 1), lines)
            return carry

        lax.fori_loop(rim, tiles - rim, rest_step, 0, unroll=2)
    for h in range(chunks):
        for k in range(count):
            sub_copy(k, h).wait_send()

    def partial(first, last):
        left = basis[:, :, halo + first * rows : halo + last * rows]
        right = image[:, :, first * rows : last * rows]
        return dot_nt(left.reshape(columns, -1), right.reshape(columns, -1))

    for h in range(chunks):
        if h == chunks - 1:
            part[...] = partial(rim, tiles - rim)
        wait_pair(rim_copy(h))
        for t in edges:
            image_of(t, slice(1, slots + 1), slice(h * depth, (h + 1) * depth))
    total = part[...] + partial(0, rim) + partial(tiles - rim, tiles)
    part_low[...] = total.astype(part_low.dtype)
    part[...] = total

    red_copies = []
    for step in range(1, layers):
        peer = lax.rem(g + step, layers)
        red_copies.append(
            pltpu.make_async_remote_copy(
                src_ref=part_low.at[pl.ds(pl.multiple_of(peer * share, share), share)],
                dst_ref=shares.at[step - 1],
                send_sem=red_send.at[step - 1],
                recv_sem=red_recv.at[step - 1],
                device_id=(s, peer),
                device_id_type=MESH,
            )
        )
    for copy in red_copies:
        copy.start()
    for copy in red_copies:
        copy.wait()
    result = part[pl.ds(pl.multiple_of(g * share, share), share), :]
    for step in range(1, layers):
        result = result + shares[step - 1].astype(jnp.float32)
    out_ref[0] = result


def on_device(subs, layers, stiffness, deflation, off_map, need_map, place_map):
    _, tiles, bands, rows, _ = stiffness.shape
    _, vectors, width = deflation.shape
    slots, overlap = place_map.shape[2:]
    columns = vectors * (slots + 1)
    halo = (bands // 2) * rows
    share = columns // layers
    count = len(OFFSETS)
    chunks = CHUNKS
    low = deflation.dtype
    dma = pltpu.SemaphoreType.DMA
    tables = (
        off_map.T,
        need_map.transpose(1, 2, 3, 0),
        place_map.transpose(0, 2, 1, 3),
    )
    return pl.pallas_call(
        functools.partial(kernel, subs, layers, chunks),
        out_shape=pltpu.VMEM((1, share, columns), jnp.float32),
        in_specs=[pl.BlockSpec(memory_space=pl.ANY)] * 5,
        out_specs=pl.BlockSpec(memory_space=pltpu.VMEM),
        scratch_shapes=[
            *[pltpu.SMEM(table.shape, table.dtype) for table in tables],
            pltpu.VMEM((tiles, bands, rows, rows), low),
            pltpu.VMEM((slots + 1, vectors, width + 2 * halo), low),
            pltpu.VMEM((slots + 1, vectors, width), low),
            pltpu.VMEM((tiles, vectors, rows), low),
            pltpu.VMEM((count, overlap, vectors, rows), low),
            pltpu.VMEM((columns, columns), jnp.float32),
            pltpu.VMEM((columns, columns), low),
            pltpu.VMEM((layers - 1, share, columns), low),
            dma((4,)),
            dma((tiles,)),
            dma((chunks, count)), dma((chunks, count)),
            dma((2,)), dma((2,)),
            dma((chunks, 2)), dma((chunks, 2)),
            dma((layers - 1,)), dma((layers - 1,)),
            *[pltpu.VMEM((count * (overlap + 1), vectors // chunks, rows), low)] * chunks,
        ],
        compiler_params=pltpu.CompilerParams(collective_id=0, has_side_effects=True),
    )(*tables, deflation, stiffness)


def solution(mesh):
    in_specs = (
        P("sub", "grp", None, None, None),
        P("sub", None, "grp"),
        P(),
        P(None, "grp", None, None),
        P("sub", "grp", None, None),
    )
    out_specs = P("sub", "grp", None)
    return jax.shard_map(
        functools.partial(on_device, mesh.shape["sub"], mesh.shape["grp"]),
        mesh=mesh,
        in_specs=in_specs,
        out_specs=out_specs,
        check_vma=False,
    )
```

time: 28.7 us -> 27.1 us (0.944)
  local copies, waits for them, and re-layouts: 1.47 us -> 0.63 us
  Pallas kernels: 27.1 us -> 26.3 us
    unnamed x1, local copies, waits for them, and re-layouts: 1.47 us -> 0.63 us
    pallas_call x1, Pallas kernels: 27.1 us -> 26.3 us  [on_device(): pl.pallas_call(functools.partial(kernel, subs, layers, chunks), out_shape...]
where the time goes in v2:
time: 27.1 us; the launch traced here: 26.9 us
  Pallas kernels  26.3 us (97%)
  local copies, waits for them, and re-layouts  0.63 us (2%)
    pallas_call x1, Pallas kernels, on_device(): pl.pallas_call(functools.partial(kernel, subs, layers, chunks), out_shape...  26.3 us
    unnamed x1, local copies, waits for them, and re-layouts  0.63 us

profile of v2, /device:TPU:0, one launch (start us, length us, event | category | flops | bytes accessed | tf_op | source)
XLA Modules:
  0.0 26.9 jit_solution(531465143706832437)
XLA Ops:
  0.0 26.3 %shard_map.55 = f32[1,64,256]{2,1,0:T(8,128)S(1)} custom-call(s32[3,8]{1,0:T(4,128)} %bitcast.4, s32[1,3,4,8]{3,2,1,0:T(4,128)} %bitcast.3, s32[1,3,1,4]{3,2,1,0:T(1,128)} %bitcast.5, bf16[1,64,4096]{2,1,0:T(8,128)(2,1)} %defl_ref.1, bf16[1,16,5,256,256]{4,3,2,1,0:T(8,128)(2,1)} %stiff_ref.1), custom_call_target="tpu_custom_call" | custom-call | tf_op jit(solution)/shard_map/pallas_call | solution.py:267
  26.3 0.6 %copy.7 = f32[1,64,256]{2,1,0:T(8,128)} copy(f32[1,64,256]{2,1,0:T(8,128)S(1)} %shard_map.55) | data formatting | bytes 131072

commit v3 on v2

--- a/solution.py
+++ b/solution.py
@@ -205,7 +205,7 @@
             image_of(t, slice(1, slots + 1), lines)
             return carry
 
-        lax.fori_loop(rim, tiles - rim, rest_step, 0, unroll=2)
+        lax.fori_loop(rim, tiles - rim, rest_step, 0, unroll=tiles - 2 * rim)
     for h in range(chunks):
         for k in range(count):
             sub_copy(k, h).wait_send()

time: 27.1 us -> 26.4 us (0.974)
  Pallas kernels: 26.3 us -> 25.7 us
    pallas_call x1, Pallas kernels: 26.3 us -> 25.7 us  [on_device(): pl.pallas_call(functools.partial(kernel, subs, layers, chunks), out_shape...]
where the time goes in v3:
time: 26.4 us; the launch traced here: 26.3 us
  Pallas kernels  25.7 us (97%)
  local copies, waits for them, and re-layouts  0.63 us (2%)
    pallas_call x1, Pallas kernels, on_device(): pl.pallas_call(functools.partial(kernel, subs, layers, chunks), out_shape...  25.7 us
    unnamed x1, local copies, waits for them, and re-layouts  0.63 us

profile of v3, /device:TPU:0, one launch (start us, length us, event | category | flops | bytes accessed | tf_op | source)
XLA Modules:
  0.0 26.3 jit_solution(15001245659846039087)
XLA Ops:
  0.0 25.7 %shard_map.55 = f32[1,64,256]{2,1,0:T(8,128)S(1)} custom-call(s32[3,8]{1,0:T(4,128)} %bitcast.4, s32[1,3,4,8]{3,2,1,0:T(4,128)} %bitcast.3, s32[1,3,1,4]{3,2,1,0:T(1,128)} %bitcast.5, bf16[1,64,4096]{2,1,0:T(8,128)(2,1)} %defl_ref.1, bf16[1,16,5,256,256]{4,3,2,1,0:T(8,128)(2,1)} %stiff_ref.1), custom_call_target="tpu_custom_call" | custom-call | tf_op jit(solution)/shard_map/pallas_call | solution.py:267
  25.7 0.6 %copy.7 = f32[1,64,256]{2,1,0:T(8,128)} copy(f32[1,64,256]{2,1,0:T(8,128)S(1)} %shard_map.55) | data formatting | bytes 131072
